TPU v7x, 128 devices: a whole 4x4x4 slice. The times are simulated.
128 devices in a mesh: row: 16 (over x, z), col: 8 (over y, core).
Axes of the slice: x: 4, y: 4, z: 4, core: 2. Of those that a mesh axis runs over, the one named last changes fastest.
Arguments:
- blocks: bfloat16 [512, 16, 128, 128], P('row', 'col'), may hold values from -0.375 to 0.375
- pattern: int32 [512, 16], replicated, may hold values from 0 to 511, as said below
- owners: int32 [8, 512, 2, 1], P('col', 'row'), may hold values from 0 to 15; in each aligned block of 64 rows (0 to 63, 64 to 127, ..., all dimensions but the last counted through in order) at most 6 rows name the same one
Outputs:
- moved: bfloat16 [8, 16, 96, 128, 128], P('col', 'row')
Inputs may be any that keep to these rules, and one draw needn't show every extreme that they name: `pattern`: block row i holds 16 distinct column blocks (i + d) mod 512, by rising d with |d| <= 8, d = 0 among them, in slot order. `owners`: among the 64 entries of one device no value occurs more than 6 times; in some device some value occurs exactly 6 times.
All inputs are finite; a program needn't handle non-finite values.
Results may differ from a plain program's by a relative error of at most 0.0049.
Values may be sent and summed in bfloat16 or wider, within the bound.
No kernel may reach another device: no remote copies, remote signals or barrier semaphores. Data moves between devices by JAX's collectives and lax.ppermute only.
A program may use at most 192 MiB of HBM per device.

v0:
```python
import math
import jax
import jax.numpy as jnp
from jax import lax
from jax.sharding import PartitionSpec as P


def extended_2(shard, sides, width):
    for axis, dim in sides:
        devices, length = (lax.axis_size(axis), shard.shape[dim])
        up = [(i, (i + 1) % devices) for i in range(devices)]
        down = [(j, i) for i, j in up]
        last = lax.slice_in_dim(shard, length - width, length, axis=dim)
        first = lax.slice_in_dim(shard, 0, width, axis=dim)
        before = lax.ppermute(last, axis, up)
        after = lax.ppermute(first, axis, down)
        shard = jnp.concatenate([before, shard, after], axis=dim)
    return shard


def local_index(pattern, start_row, row_count, margin, slot_start, target_count):
    nblk, slot_count = pattern.shape
    reach = slot_count // 2
    own_cols = lax.dynamic_slice_in_dim(pattern, start_row, row_count, 0)
    row_ids = start_row + jnp.arange(row_count, dtype=jnp.int32)
    offsets = (own_cols - row_ids[:, None] + reach + nblk) % nblk - reach
    ext_row = jnp.arange(row_count, dtype=jnp.int32)[:, None] + margin + offsets
    neighbour_cols = pattern[own_cols]
    wanted = lax.dynamic_slice_in_dim(own_cols, slot_start, target_count, 1)
    same_col = neighbour_cols[:, None, :, :] == wanted[:, :, None, None]
    has_match = jnp.any(same_col, axis=-1)
    match_slot = jnp.sum(
        same_col.astype(jnp.int32) * jnp.arange(slot_count, dtype=jnp.int32), axis=-1
    )
    extent = (row_count + 2 * margin) * slot_count
    return jnp.where(has_match, ext_row[:, None, :] * slot_count + match_slot, extent)


def multiply(left, extended, pick_index):
    row_count, slot_count, tile_size = (left.shape[0], left.shape[1], left.shape[-1])
    target_count = pick_index.shape[1]
    group_rows = math.gcd(row_count, max(1, 32 // target_count))
    flat_table = jnp.concatenate(
        [
            extended.reshape(-1, tile_size, tile_size),
            jnp.zeros((1, tile_size, tile_size), extended.dtype),
        ],
        axis=0,
    )

    def per_group(operands):
        left_rows, pick_rows = operands
        picked = flat_table[pick_rows]
        return jnp.einsum("gtab,gstbc->gsac", left_rows, picked, preferred_element_type=jnp.float32)

    result = lax.map(
        per_group,
        (
            left.reshape(row_count // group_rows, group_rows, slot_count, tile_size, tile_size),
            pick_index.reshape(row_count // group_rows, group_rows, target_count, slot_count),
        ),
    )
    return result.reshape(row_count, target_count, tile_size, tile_size)


def per_device(blocks, pattern, owners):
    row_count, slot_share, tile_size = (blocks.shape[0], blocks.shape[1], blocks.shape[-1])
    slot_count = pattern.shape[1]
    reach = slot_count // 2
    row_pos = lax.axis_index("row")
    col_pos = lax.axis_index("col")
    row_devices = lax.axis_size("row")
    full_rows = lax.all_gather(blocks, "col", axis=1, tiled=True)
    extended = extended_2(full_rows, (("row", 0),), reach)
    pick_index = local_index(
        pattern, row_pos * row_count, row_count, reach, col_pos * slot_share, slot_share
    )
    squared = multiply(full_rows, extended, pick_index).astype(jnp.bfloat16)
    square_rows = lax.all_gather(squared, "col", axis=1, tiled=True)
    cube_term = multiply(square_rows, extended, pick_index)
    result = (3.0 * squared.astype(jnp.float32) - 2.0 * cube_term).astype(jnp.bfloat16)
    block_count = row_count * slot_share
    capacity = 3 * block_count // (2 * row_devices)
    flat_result = result.reshape(block_count, tile_size, tile_size)
    destination = owners.reshape(block_count)
    one_hot = (destination[:, None] == jnp.arange(row_devices, dtype=jnp.int32)[None, :]).astype(
        jnp.int32
    )
    bucket_rank = jnp.sum((jnp.cumsum(one_hot, axis=0) - 1) * one_hot, axis=1)
    bucket_slot = destination * capacity + bucket_rank
    wanted = jnp.arange(row_devices * capacity, dtype=jnp.int32)
    slot_match = bucket_slot[None, :] == wanted[:, None]
    has_source = jnp.any(slot_match, axis=1)
    source = jnp.sum(
        slot_match.astype(jnp.int32) * jnp.arange(block_count, dtype=jnp.int32)[None, :], axis=1
    )
    padded = jnp.concatenate(
        [flat_result, jnp.zeros((1, tile_size, tile_size), flat_result.dtype)], axis=0
    )
    buckets = padded[jnp.where(has_source, source, block_count)].reshape(
        row_devices, capacity, tile_size, tile_size
    )
    received = lax.all_to_all(buckets, "row", split_axis=0, concat_axis=0, tiled=True)
    return received.reshape(1, 1, row_devices * capacity, tile_size, tile_size)


def solution(mesh):
    in_specs = (P("row", "col", None, None), P(), P("col", "row", None, None))
    out_specs = P("col", "row", None, None, None)
    return jax.shard_map(
        per_device, mesh=mesh, in_specs=in_specs, out_specs=out_specs, check_vma=False
    )
```

profile of v0, /device:TPU:8, one launch (start us, length us, event | category | flops | bytes accessed | tf_op | source)
XLA Modules:
  0.0 546.1 jit_solution(1662284565458652383)
XLA Ops:
  7.3 88.5 %all-gather.3.cloned.1.call-done = bf16[32,16,128,128]{3,2,1,0:T(8,128)(2,1)} async-done(((bf16[32,2,128,128]{3,2,1,0:T(8,128)(2,1)}), bf16[32,16,128,128]{3,2,1,0:T(8,128)(2,1)}) %all-gather.3.cloned.1.call-update) | async-done | bytes 16777232 | tf_op jit(solution)/shard_map/all_gather | solution.py:73
  95.9 6.0 %fusion.20 = (bf16[8,16,128,128]{3,2,1,0:T(8,128)(2,1)}, bf16[8,16,128,128]{3,2,1,0:T(8,128)(2,1)}) fusion(bf16[32,16,128,128]{3,2,1,0:T(8,128)(2,1)} %all-gather.3.cloned.1.call-done), kind=kLoop, calls=%fused_computation.45 | loop fusion | bytes 16777216 | tf_op jit(solution)/shard_map/slice | solution.py:13
  101.9 1.6 collective-permute-start
  103.4 3.8 collective-permute-start.1
  109.9 88.4 %collective-permute-done = bf16[8,16,128,128]{3,2,1,0:T(8,128)(2,1)} collective-permute-done((bf16[8,16,128,128]{3,2,1,0:T(8,128)(2,1)}, bf16[8,16,128,128]{3,2,1,0:T(8,128)(2,1)}, u32[]{:S(2)}, u32[]{:S(2)}) %collective-permute-start) | collective-permute-done | bytes 4194336 | tf_op jit(solution)/shard_map/ppermute | solution.py:15
  198.3 17.7 %pad_maximum_fusion = bf16[48,16,128,128]{3,2,1,0:T(8,128)(2,1)} fusion(bf16[8,16,128,128]{3,2,1,0:T(8,128)(2,1)} %collective-permute-done.1, bf16[32,16,128,128]{3,2,1,0:T(8,128)(2,1)} %all-gather.3.cloned.1.call-done, bf16[8,16,128,128]{3,2,1,0:T(8,128)(2,1)} %collective-permute-done), kind=kLoop, calls=%fused_computation.18 | loop fusion | flops 25165824 | bytes 50331648 | tf_op jit(solution)/shard_map/concatenate | solution.py:17
  216.0 22.0 %concatenate.11 = bf16[769,128,128]{2,1,0:T(8,128)(2,1)} pad(bf16[768,128,128]{2,1,0:T(8,128)(2,1)} %bitcast.93, bf16[]{:T(256)} %constant.99.clone.1), padding=0_1x0_0x0_0 | pad | bytes 50364416 | tf_op jit(solution)/shard_map/concatenate | solution.py:43
  237.9 66.3 %while.22 = (s32[]{:T(128)}, bf16[2,16,2,128,128]{3,4,2,1,0:T(8,128)(2,1)S(1)}, s32[2,16,2,16]{3,2,1,0:T(2,128)S(1)}, bf16[769,128,128]{2,1,0:T(8,128)(2,1)}, bf16[2,16,16,128,128]{4,3,2,1,0:T(8,128)(2,1)}) while((s32[]{:T(128)}, bf16[2,16,2,128,128]{3,4,2,1,0:T(8,128)(2,1)S(1)}, s32[2,16,2,16]{3,2,1,0:T(2,128)S(1)}, ...), condition=%wide.region_3.4_spmd.clone, body=%wide.region_2.3_spmd.sunk.clone | while | flops 2147486208 | bytes 60834880 | solution.py:56
  238.1 21.9 %gather_fusion = bf16[512,128,128]{2,1,0:T(8,128)(2,1)} fusion(bf16[769,128,128]{2,1,0:T(8,128)(2,1)} %get-tuple-element.196, s32[1024]{0:T(1024)S(1)} %pad_clamp_fusion.8), kind=kCustom, calls=%fused_computation.clone.1.clone | custom fusion | bytes 33556480 | tf_op jit(solution)/shard_map/while/body/eval_jaxpr/gather | solution.py:53
  259.9 11.2 %bitcast_dynamic-update-slice_fusion.6 = bf16[2,16,2,128,128]{3,4,2,1,0:T(8,128)(2,1)S(1)} fusion(bf16[2,16,2,128,128]{3,4,2,1,0:T(8,128)(2,1)S(1)} %get-tuple-element.189, s32[]{:T(128)} %get-tuple-element.188, bf16[16,2,16,128,128]{4,3,2,1,0:T(8,128)(2,1)} %bitcast.91, bf16[2,16,16,128,128]{4,3,2,1,0:T(8,128)(2,1)} %get-tuple-element.197), kind=kOutput, calls=%fused_computation.7.clone.1.clone | convolution fusion | flops 2147483648 | bytes 27264000 | tf_op jit(solution)/shard_map/while/body/eval_jaxpr/gtab,gstbc->gsac/dot_general | solution.py:54
  271.2 21.9 %gather_fusion = bf16[512,128,128]{2,1,0:T(8,128)(2,1)} fusion(bf16[769,128,128]{2,1,0:T(8,128)(2,1)} %get-tuple-element.196, s32[1024]{0:T(1024)S(1)} %pad_clamp_fusion.8), kind=kCustom, calls=%fused_computation.clone.1.clone | custom fusion | bytes 33556480 | tf_op jit(solution)/shard_map/while/body/eval_jaxpr/gather | solution.py:53
  293.1 11.2 %bitcast_dynamic-update-slice_fusion.6 = bf16[2,16,2,128,128]{3,4,2,1,0:T(8,128)(2,1)S(1)} fusion(bf16[2,16,2,128,128]{3,4,2,1,0:T(8,128)(2,1)S(1)} %get-tuple-element.189, s32[]{:T(128)} %get-tuple-element.188, bf16[16,2,16,128,128]{4,3,2,1,0:T(8,128)(2,1)} %bitcast.91, bf16[2,16,16,128,128]{4,3,2,1,0:T(8,128)(2,1)} %get-tuple-element.197), kind=kOutput, calls=%fused_computation.7.clone.1.clone | convolution fusion | flops 2147483648 | bytes 27264000 | tf_op jit(solution)/shard_map/while/body/eval_jaxpr/gtab,gstbc->gsac/dot_general | solution.py:54
  306.4 84.6 %all-gather.5.cloned.1.call-done = bf16[32,16,128,128]{2,3,1,0:T(8,128)(2,1)} async-done(((bf16[32,2,128,128]{2,3,1,0:T(8,128)(2,1)}), bf16[32,16,128,128]{2,3,1,0:T(8,128)(2,1)}) %all-gather.5.cloned.1.call-update) | async-done | bytes 16777232 | tf_op jit(solution)/shard_map/all_gather | solution.py:79
  391.1 22.5 %copy.41 = bf16[32,16,128,128]{3,2,1,0:T(8,128)(2,1)} copy(bf16[32,16,128,128]{2,3,1,0:T(8,128)(2,1)} %all-gather.5.cloned.1.call-done) | data formatting | bytes 33554432 | tf_op jit(solution)/shard_map/all_gather | solution.py:79
  413.6 67.6 %while.23 = (s32[]{:T(128)}, f32[2,16,2,128,128]{3,4,2,1,0:T(8,128)}, s32[2,16,2,16]{3,2,1,0:T(2,128)S(1)}, bf16[769,128,128]{2,1,0:T(8,128)(2,1)}, bf16[2,16,16,128,128]{4,3,2,1,0:T(8,128)(2,1)}) while((s32[]{:T(128)}, f32[2,16,2,128,128]{3,4,2,1,0:T(8,128)}, s32[2,16,2,16]{3,2,1,0:T(2,128)S(1)}, ...), condition=%wide.region_5.6_spmd.clone, body=%wide.region_4.5_spmd.sunk.clone | while | flops 2147486208 | bytes 60834880 | solution.py:56
  413.7 22.0 %gather_fusion.1 = bf16[512,128,128]{2,1,0:T(8,128)(2,1)} fusion(bf16[769,128,128]{2,1,0:T(8,128)(2,1)} %get-tuple-element.211, s32[1024]{0:T(1024)S(1)} %pad_clamp_fusion.9), kind=kCustom, calls=%fused_computation.1.clone.1.clone | custom fusion | bytes 33556480 | tf_op jit(solution)/shard_map/while/body/eval_jaxpr/gather | solution.py:53
  435.7 11.7 %bitcast_dynamic-update-slice_fusion.7 = f32[2,16,2,128,128]{3,4,2,1,0:T(8,128)} fusion(f32[2,16,2,128,128]{3,4,2,1,0:T(8,128)} %get-tuple-element.204, s32[]{:T(128)} %get-tuple-element.203, bf16[16,2,16,128,128]{4,3,2,1,0:T(8,128)(2,1)} %bitcast.92, bf16[2,16,16,128,128]{4,3,2,1,0:T(8,128)(2,1)} %get-tuple-element.212), kind=kOutput, calls=%fused_computation.14.clone.1.clone | convolution fusion | flops 2147483648 | bytes 27264000 | tf_op jit(solution)/shard_map/while/body/eval_jaxpr/gtab,gstbc->gsac/dot_general | solution.py:54
  447.5 21.9 %gather_fusion.1 = bf16[512,128,128]{2,1,0:T(8,128)(2,1)} fusion(bf16[769,128,128]{2,1,0:T(8,128)(2,1)} %get-tuple-element.211, s32[1024]{0:T(1024)S(1)} %pad_clamp_fusion.9), kind=kCustom, calls=%fused_computation.1.clone.1.clone | custom fusion | bytes 33556480 | tf_op jit(solution)/shard_map/while/body/eval_jaxpr/gather | solution.py:53
  469.4 11.8 %bitcast_dynamic-update-slice_fusion.7 = f32[2,16,2,128,128]{3,4,2,1,0:T(8,128)} fusion(f32[2,16,2,128,128]{3,4,2,1,0:T(8,128)} %get-tuple-element.204, s32[]{:T(128)} %get-tuple-element.203, bf16[16,2,16,128,128]{4,3,2,1,0:T(8,128)(2,1)} %bitcast.92, bf16[2,16,16,128,128]{4,3,2,1,0:T(8,128)(2,1)} %get-tuple-element.212), kind=kOutput, calls=%fused_computation.14.clone.1.clone | convolution fusion | flops 2147483648 | bytes 27264000 | tf_op jit(solution)/shard_map/while/body/eval_jaxpr/gtab,gstbc->gsac/dot_general | solution.py:54
  481.2 2.9 subtract_convert_fusion
  484.3 2.7 gather_fusion.3
  487.0 3.5 copy.44
  490.5 47.1 %all_to_all.5 = bf16[16,6,128,128]{3,2,1,0:T(8,128)(2,1)S(1)} all-to-all(bf16[16,6,128,128]{3,2,1,0:T(8,128)(2,1)S(1)} %bitcast.97), channel_id=1, replica_groups=mesh['row'=16,'col'=8] {'row'}, dimensions={0} | all-to-all | bytes 6291456 | tf_op jit(solution)/shard_map/all_to_all | solution.py:103
  537.6 1.7 copy.69
  (54 shorter events, 6.0 us)
Async XLA Ops:
  6.5 89.3 %all-gather.3.cloned.1.call-start = ((), (), s32[]{:S(2)}) async-start(), calls=%async_computation.1 | async-start | bytes 18874368 | tf_op jit(solution)/shard_map/all_gather | solution.py:73
  7.3 100.0 %copy-start.2 = (s32[512,16]{0,1:T(8,128)S(1)}, s32[512,16]{0,1:T(8,128)}, u32[]{:S(2)}) copy-start(s32[512,16]{0,1:T(8,128)} %param.8) | copy-start | bytes 98308
  7.3 383.8 %all-gather.5.cloned.1.call-start = ((), (), s32[]{:S(2)}) async-start(), calls=%async_computation.2 | async-start | bytes 18874368 | tf_op jit(solution)/shard_map/all_gather | solution.py:79
  101.9 96.4 %collective-permute-start = (bf16[8,16,128,128]{3,2,1,0:T(8,128)(2,1)}, bf16[8,16,128,128]{3,2,1,0:T(8,128)(2,1)}, u32[]{:S(2)}, u32[]{:S(2)}) collective-permute-start(bf16[8,16,128,128]{3,2,1,0:T(8,128)(2,1)} %get-tuple-element.91), channel_id=1, source_target_pairs={{0,8},{8,16},{16,24},{24,32},{32,40},{40,48},{48,56},{56,64},{64,7... | collective-permute-start | bytes 12582920 | tf_op jit(solution)/shard_map/ppermute | solution.py:15
  103.4 94.8 %collective-permute-start.1 = (bf16[8,16,128,128]{3,2,1,0:T(8,128)(2,1)}, bf16[8,16,128,128]{3,2,1,0:T(8,128)(2,1)}, u32[]{:S(2)}, u32[]{:S(2)}) collective-permute-start(bf16[8,16,128,128]{3,2,1,0:T(8,128)(2,1)} %get-tuple-element.92), channel_id=1, source_target_pairs={{8,0},{16,8},{24,16},{32,24},{40,32},{48,40},{56,48},{64,56},{72,6... | collective-permute-start | bytes 12582920 | tf_op jit(solution)/shard_map/ppermute | solution.py:16
  237.9 67.7 %copy-start.3 = (s32[1,32,2,1]{1,3,2,0:T(1,128)S(1)}, s32[1,32,2,1]{1,3,2,0:T(1,128)}, u32[]{:S(2)}) copy-start(s32[1,32,2,1]{1,3,2,0:T(1,128)} %param.9) | copy-start | bytes 772
  304.3 1.3 copy-start
  413.6 67.6 %copy-start.1 = (bf16[2,16,2,128,128]{3,4,2,1,0:T(8,128)(2,1)S(1)}, bf16[2,16,2,128,128]{3,4,2,1,0:T(8,128)(2,1)}, u32[]{:S(2)}) copy-start(bf16[2,16,2,128,128]{3,4,2,1,0:T(8,128)(2,1)} %copy-done) | copy-start | bytes 6291460
Sparse Core Ops, SparseCore 0:
  9.0 86.7 all-gather.2
  305.8 85.2 all-gather.4
where the time goes:
time: 547 us; the launch traced here: 546 us
  waiting for transfers between devices  262 us (48%)
  local copies, waits for them, and re-layouts  150 us (27%)
  blocking collectives  47.1 us (9%)
  matrix products  45.9 us (8%)
  other arithmetic  22 us (4%)
  between operations  13.6 us (2%)
    all_gather x1, waiting for transfers between devices, per_device(): full_rows = lax.all_gather(blocks, 'col', axis=1, tiled=True)  88.5 us
    ppermute x1, waiting for transfers between devices, extended_2(): before = lax.ppermute(last, axis, up)  88.4 us
    gather x4, local copies, waits for them, and re-layouts, per_group(): picked = flat_table[pick_rows]  87.6 us
    all_gather x1, waiting for transfers between devices, per_device(): square_rows = lax.all_gather(squared, 'col', axis=1, tiled=True)  84.6 us
    all_to_all x1, blocking collectives, per_device(): lax.all_to_all(buckets, 'row', split_axis=0, concat_axis=0, tiled=True)  47.1 us
    dot_general x4, matrix products, per_group(): jnp.einsum('gtab,gstbc->gsac', left_rows, picked, preferred_element_type=...  45.9 us
    all_gather x1, local copies, waits for them, and re-layouts, per_device(): square_rows = lax.all_gather(squared, 'col', axis=1, tiled=True)  22.5 us
    concatenate x1, local copies, waits for them, and re-layouts, multiply(): jnp.concatenate([extended.reshape(-1, tile_size, tile_size), jnp.zeros((1...  22 us
  transfers between devices with their start and end apart: 4, of which 3 were waited for; matrix products, arithmetic and copies ran while one was open for 1% of the time, Pallas kernels for 0%

commit v1 on v0

--- a/solution.py
+++ b/solution.py
@@ -70,7 +70,20 @@
     row_pos = lax.axis_index("row")
     col_pos = lax.axis_index("col")
     row_devices = lax.axis_size("row")
-    full_rows = lax.all_gather(blocks, "col", axis=1, tiled=True)
+
+    def bind_the_tiles(dim_k, x_local):
+        p_next = jnp.concatenate(
+            jax.lax.all_to_all(
+                jnp.stack(jax.lax.axis_size("col") * [x_local]),
+                axis_name="col",
+                split_axis=0,
+                concat_axis=0,
+            ),
+            axis=dim_k,
+        )
+        return p_next
+
+    full_rows = bind_the_tiles(1, x_local=blocks)
     extended = extended_2(full_rows, (("row", 0),), reach)
     pick_index = local_index(
         pattern, row_pos * row_count, row_count, reach, col_pos * slot_share, slot_share

time: 547 us -> 657 us (1.20)
  blocking collectives: 47.1 us -> 237 us
  waiting for transfers between devices: 262 us -> 172 us
  local copies, waits for them, and re-layouts: 150 us -> 159 us
    all_to_all x0 -> x1, blocking collectives: none -> 190 us  [bind_the_tiles(): jax.lax.all_to_all(jnp.stack(jax.lax.axis_size('col') * [x_local]), axis_...]
    all_gather x1 -> x0, waiting for transfers between devices: 88.5 us -> none  [per_device(): full_rows = lax.all_gather(blocks, 'col', axis=1, tiled=True)]
  transfers between devices with their start and end apart: 4 -> 3, of which waited for: 3 -> 2; matrix products, arithmetic and copies ran while one was open for 1% -> 1% of each run, Pallas kernels for 0% -> 0%
where the time goes in v1:
time: 657 us; the launch traced here: 656 us
  blocking collectives  237 us (36%)
  waiting for transfers between devices  172 us (26%)
  local copies, waits for them, and re-layouts  159 us (24%)
  matrix products  45.9 us (7%)
  other arithmetic  22 us (3%)
  between operations  13.6 us (2%)
    all_to_all x1, blocking collectives, bind_the_tiles(): jax.lax.all_to_all(jnp.stack(jax.lax.axis_size('col') * [x_local]), axis_...  190 us
    ppermute x1, waiting for transfers between devices, extended_2(): before = lax.ppermute(last, axis, up)  87.9 us
    gather x4, local copies, waits for them, and re-layouts, per_group(): picked = flat_table[pick_rows]  87.6 us
    all_gather x1, waiting for transfers between devices, per_device(): square_rows = lax.all_gather(squared, 'col', axis=1, tiled=True)  84.1 us
    all_to_all x1, blocking collectives, per_device(): lax.all_to_all(buckets, 'row', split_axis=0, concat_axis=0, tiled=True)  47.1 us
    dot_general x4, matrix products, per_group(): jnp.einsum('gtab,gstbc->gsac', left_rows, picked, preferred_element_type=...  45.9 us
    all_gather x1, local copies, waits for them, and re-layouts, per_device(): square_rows = lax.all_gather(squared, 'col', axis=1, tiled=True)  22.5 us
    concatenate x1, local copies, waits for them, and re-layouts, multiply(): jnp.concatenate([extended.reshape(-1, tile_size, tile_size), jnp.zeros((1...  22 us
  transfers between devices with their start and end apart: 3, of which 2 were waited for; matrix products, arithmetic and copies ran while one was open for 1% of the time, Pallas kernels for 0%

profile of v1, /device:TPU:8, one launch (start us, length us, event | category | flops | bytes accessed | tf_op | source)
XLA Modules:
  0.0 656.2 jit_solution(3914525302599215496)
XLA Ops:
  6.5 5.1 stack.2
  11.7 190.1 %all_to_all.10 = bf16[8,32,2,128,128]{4,3,2,1,0:T(8,128)(2,1)S(1)} all-to-all(bf16[8,32,2,128,128]{4,3,2,1,0:T(8,128)(2,1)S(1)} %stack.2), channel_id=1, replica_groups=mesh['row'=16,'col'=8] {'col'}, dimensions={0} | all-to-all | bytes 33554432 | tf_op jit(solution)/shard_map/all_to_all | solution.py:76
  204.0 4.1 fusion.20
  208.0 4.1 copy-done
  214.1 4.3 collective-permute-start.1
  221.0 87.9 %collective-permute-done = bf16[8,16,128,128]{3,2,1,0:T(8,128)(2,1)} collective-permute-done((bf16[8,16,128,128]{3,2,1,0:T(8,128)(2,1)}, bf16[8,16,128,128]{3,2,1,0:T(8,128)(2,1)}, u32[]{:S(2)}, u32[]{:S(2)}) %collective-permute-start) | collective-permute-done | bytes 4194336 | tf_op jit(solution)/shard_map/ppermute | solution.py:15
  308.9 17.7 %pad_maximum_fusion = bf16[48,16,128,128]{3,2,1,0:T(8,128)(2,1)} fusion(bf16[8,16,128,128]{3,2,1,0:T(8,128)(2,1)} %collective-permute-done.1, bf16[32,16,128,128]{3,2,1,0:T(8,128)(2,1)} %bitcast.101, bf16[8,16,128,128]{3,2,1,0:T(8,128)(2,1)} %collective-permute-done), kind=kLoop, calls=%fused_computation.18 | loop fusion | flops 25165824 | bytes 50331648 | tf_op jit(solution)/shard_map/concatenate | solution.py:17
  326.6 22.0 %concatenate.11 = bf16[769,128,128]{2,1,0:T(8,128)(2,1)} pad(bf16[768,128,128]{2,1,0:T(8,128)(2,1)} %bitcast.103, bf16[]{:T(256)} %constant.99.clone.1), padding=0_1x0_0x0_0 | pad | bytes 50364416 | tf_op jit(solution)/shard_map/concatenate | solution.py:43
  348.6 66.3 %while.22 = (s32[]{:T(128)}, bf16[2,16,2,128,128]{3,4,2,1,0:T(8,128)(2,1)S(1)}, s32[2,16,2,16]{3,2,1,0:T(2,128)S(1)}, bf16[769,128,128]{2,1,0:T(8,128)(2,1)}, bf16[2,16,16,128,128]{4,3,2,1,0:T(8,128)(2,1)}) while((s32[]{:T(128)}, bf16[2,16,2,128,128]{3,4,2,1,0:T(8,128)(2,1)S(1)}, s32[2,16,2,16]{3,2,1,0:T(2,128)S(1)}, ...), condition=%wide.region_3.4_spmd.clone, body=%wide.region_2.3_spmd.sunk.clone | while | flops 2147486208 | bytes 60834880 | solution.py:56
  348.7 21.9 %gather_fusion = bf16[512,128,128]{2,1,0:T(8,128)(2,1)} fusion(bf16[769,128,128]{2,1,0:T(8,128)(2,1)} %get-tuple-element.198, s32[1024]{0:T(1024)S(1)} %pad_clamp_fusion.8), kind=kCustom, calls=%fused_computation.clone.1.clone | custom fusion | bytes 33556480 | tf_op jit(solution)/shard_map/while/body/eval_jaxpr/gather | solution.py:53
  370.5 11.2 %bitcast_dynamic-update-slice_fusion.6 = bf16[2,16,2,128,128]{3,4,2,1,0:T(8,128)(2,1)S(1)} fusion(bf16[2,16,2,128,128]{3,4,2,1,0:T(8,128)(2,1)S(1)} %get-tuple-element.191, s32[]{:T(128)} %get-tuple-element.190, bf16[16,2,16,128,128]{4,3,2,1,0:T(8,128)(2,1)} %bitcast.98, bf16[2,16,16,128,128]{4,3,2,1,0:T(8,128)(2,1)} %get-tuple-element.199), kind=kOutput, calls=%fused_computation.7.clone.1.clone | convolution fusion | flops 2147483648 | bytes 27264000 | tf_op jit(solution)/shard_map/while/body/eval_jaxpr/gtab,gstbc->gsac/dot_general | solution.py:54
  381.9 21.9 %gather_fusion = bf16[512,128,128]{2,1,0:T(8,128)(2,1)} fusion(bf16[769,128,128]{2,1,0:T(8,128)(2,1)} %get-tuple-element.198, s32[1024]{0:T(1024)S(1)} %pad_clamp_fusion.8), kind=kCustom, calls=%fused_computation.clone.1.clone | custom fusion | bytes 33556480 | tf_op jit(solution)/shard_map/while/body/eval_jaxpr/gather | solution.py:53
  403.7 11.2 %bitcast_dynamic-update-slice_fusion.6 = bf16[2,16,2,128,128]{3,4,2,1,0:T(8,128)(2,1)S(1)} fusion(bf16[2,16,2,128,128]{3,4,2,1,0:T(8,128)(2,1)S(1)} %get-tuple-element.191, s32[]{:T(128)} %get-tuple-element.190, bf16[16,2,16,128,128]{4,3,2,1,0:T(8,128)(2,1)} %bitcast.98, bf16[2,16,16,128,128]{4,3,2,1,0:T(8,128)(2,1)} %get-tuple-element.199), kind=kOutput, calls=%fused_computation.7.clone.1.clone | convolution fusion | flops 2147483648 | bytes 27264000 | tf_op jit(solution)/shard_map/while/body/eval_jaxpr/gtab,gstbc->gsac/dot_general | solution.py:54
  417.1 84.1 %all-gather.2.cloned.1.call-done = bf16[32,16,128,128]{2,3,1,0:T(8,128)(2,1)} async-done(((bf16[32,2,128,128]{2,3,1,0:T(8,128)(2,1)}), bf16[32,16,128,128]{2,3,1,0:T(8,128)(2,1)}) %all-gather.2.cloned.1.call-update) | async-done | bytes 16777232 | tf_op jit(solution)/shard_map/all_gather | solution.py:92
  501.1 22.5 %copy.62 = bf16[32,16,128,128]{3,2,1,0:T(8,128)(2,1)} copy(bf16[32,16,128,128]{2,3,1,0:T(8,128)(2,1)} %all-gather.2.cloned.1.call-done) | data formatting | bytes 33554432 | tf_op jit(solution)/shard_map/all_gather | solution.py:92
  523.7 67.6 %while.23 = (s32[]{:T(128)}, f32[2,16,2,128,128]{3,4,2,1,0:T(8,128)}, s32[2,16,2,16]{3,2,1,0:T(2,128)S(1)}, bf16[769,128,128]{2,1,0:T(8,128)(2,1)}, bf16[2,16,16,128,128]{4,3,2,1,0:T(8,128)(2,1)}) while((s32[]{:T(128)}, f32[2,16,2,128,128]{3,4,2,1,0:T(8,128)}, s32[2,16,2,16]{3,2,1,0:T(2,128)S(1)}, ...), condition=%wide.region_5.6_spmd.clone, body=%wide.region_4.5_spmd.sunk.clone | while | flops 2147486208 | bytes 60834880 | solution.py:56
  523.8 22.0 %gather_fusion.1 = bf16[512,128,128]{2,1,0:T(8,128)(2,1)} fusion(bf16[769,128,128]{2,1,0:T(8,128)(2,1)} %get-tuple-element.213, s32[1024]{0:T(1024)S(1)} %pad_clamp_fusion.9), kind=kCustom, calls=%fused_computation.1.clone.1.clone | custom fusion | bytes 33556480 | tf_op jit(solution)/shard_map/while/body/eval_jaxpr/gather | solution.py:53
  545.8 11.7 %bitcast_dynamic-update-slice_fusion.7 = f32[2,16,2,128,128]{3,4,2,1,0:T(8,128)} fusion(f32[2,16,2,128,128]{3,4,2,1,0:T(8,128)} %get-tuple-element.206, s32[]{:T(128)} %get-tuple-element.205, bf16[16,2,16,128,128]{4,3,2,1,0:T(8,128)(2,1)} %bitcast.99, bf16[2,16,16,128,128]{4,3,2,1,0:T(8,128)(2,1)} %get-tuple-element.214), kind=kOutput, calls=%fused_computation.14.clone.1.clone | convolution fusion | flops 2147483648 | bytes 27264000 | tf_op jit(solution)/shard_map/while/body/eval_jaxpr/gtab,gstbc->gsac/dot_general | solution.py:54
  557.6 21.9 %gather_fusion.1 = bf16[512,128,128]{2,1,0:T(8,128)(2,1)} fusion(bf16[769,128,128]{2,1,0:T(8,128)(2,1)} %get-tuple-element.213, s32[1024]{0:T(1024)S(1)} %pad_clamp_fusion.9), kind=kCustom, calls=%fused_computation.1.clone.1.clone | custom fusion | bytes 33556480 | tf_op jit(solution)/shard_map/while/body/eval_jaxpr/gather | solution.py:53
  579.5 11.8 %bitcast_dynamic-update-slice_fusion.7 = f32[2,16,2,128,128]{3,4,2,1,0:T(8,128)} fusion(f32[2,16,2,128,128]{3,4,2,1,0:T(8,128)} %get-tuple-element.206, s32[]{:T(128)} %get-tuple-element.205, bf16[16,2,16,128,128]{4,3,2,1,0:T(8,128)(2,1)} %bitcast.99, bf16[2,16,16,128,128]{4,3,2,1,0:T(8,128)(2,1)} %get-tuple-element.214), kind=kOutput, calls=%fused_computation.14.clone.1.clone | convolution fusion | flops 2147483648 | bytes 27264000 | tf_op jit(solution)/shard_map/while/body/eval_jaxpr/gtab,gstbc->gsac/dot_general | solution.py:54
  591.2 2.9 subtract_convert_fusion
  594.4 2.7 gather_fusion.3
  597.1 3.5 copy.65
  600.6 47.1 %all_to_all.11 = bf16[16,6,128,128]{3,2,1,0:T(8,128)(2,1)S(1)} all-to-all(bf16[16,6,128,128]{3,2,1,0:T(8,128)(2,1)S(1)} %bitcast.106), channel_id=1, replica_groups=mesh['row'=16,'col'=8] {'row'}, dimensions={0} | all-to-all | bytes 6291456 | tf_op jit(solution)/shard_map/all_to_all | solution.py:116
  (56 shorter events, 11.1 us)
Async XLA Ops:
  6.5 494.6 %all-gather.2.cloned.1.call-start = ((), (), s32[]{:S(2)}) async-start(), calls=%async_computation.2 | async-start | bytes 18874368 | tf_op jit(solution)/shard_map/all_gather | solution.py:92
  203.9 8.2 %copy-start = (bf16[8,32,2,128,128]{4,3,2,0,1:T(8,128)(2,1)}, bf16[8,32,2,128,128]{4,3,2,0,1:T(8,128)(2,1)S(1)}, u32[]{:S(2)}) copy-start(bf16[8,32,2,128,128]{4,3,2,0,1:T(8,128)(2,1)S(1)} %copy.76) | copy-start | bytes 50331652
  203.9 14.4 %copy-start.3 = (s32[512,16]{0,1:T(8,128)S(1)}, s32[512,16]{0,1:T(8,128)}, u32[]{:S(2)}) copy-start(s32[512,16]{0,1:T(8,128)} %param.8) | copy-start | bytes 98308
  212.1 96.8 %collective-permute-start = (bf16[8,16,128,128]{3,2,1,0:T(8,128)(2,1)}, bf16[8,16,128,128]{3,2,1,0:T(8,128)(2,1)}, u32[]{:S(2)}, u32[]{:S(2)}) collective-permute-start(bf16[8,16,128,128]{3,2,1,0:T(8,128)(2,1)} %bitcast.23), channel_id=1, source_target_pairs={{0,8},{8,16},{16,24},{24,32},{32,40},{40,48},{48,56},{56,64},{64,7... | collective-permute-start | bytes 12582920 | tf_op jit(solution)/shard_map/ppermute | solution.py:15
  214.1 94.8 %collective-permute-start.1 = (bf16[8,16,128,128]{3,2,1,0:T(8,128)(2,1)}, bf16[8,16,128,128]{3,2,1,0:T(8,128)(2,1)}, u32[]{:S(2)}, u32[]{:S(2)}) collective-permute-start(bf16[8,16,128,128]{3,2,1,0:T(8,128)(2,1)} %bitcast.25), channel_id=1, source_target_pairs={{8,0},{16,8},{24,16},{32,24},{40,32},{48,40},{56,48},{64,56},{72,6... | collective-permute-start | bytes 12582920 | tf_op jit(solution)/shard_map/ppermute | solution.py:16
  348.6 67.7 %copy-start.4 = (s32[1,32,2,1]{1,3,2,0:T(1,128)S(1)}, s32[1,32,2,1]{1,3,2,0:T(1,128)}, u32[]{:S(2)}) copy-start(s32[1,32,2,1]{1,3,2,0:T(1,128)} %param.9) | copy-start | bytes 772
  414.9 1.3 copy-start.1
  523.7 67.6 %copy-start.2 = (bf16[2,16,2,128,128]{3,4,2,1,0:T(8,128)(2,1)S(1)}, bf16[2,16,2,128,128]{3,4,2,1,0:T(8,128)(2,1)}, u32[]{:S(2)}) copy-start(bf16[2,16,2,128,128]{3,4,2,1,0:T(8,128)(2,1)} %copy-done.1) | copy-start | bytes 6291460
Sparse Core Ops, SparseCore 0:
  416.4 84.6 all-gather.1
